TPU v7x, 128 devices: a whole 4x4x4 slice. The times are simulated.
128 devices in a mesh: blk: 128 (over z, x, y, core).
Axes of the slice: x: 4, y: 4, z: 4, core: 2. Of those that a mesh axis runs over, the one named last changes fastest.
Arguments:
- state: float32 [4, 2048, 128, 256], P(None, 'blk'), may hold values from -6 to 6
- sample_cell: int32 [65536], P('blk'), may hold values from 0 to 491262, as said below
- sample_frac: float32 [3, 65536], P(None, 'blk'), may hold values from 0 to 1
- sample_owner: int32 [65536, 1], P('blk'), may hold values from 0 to 127; in each aligned block of 512 rows (0 to 511, 512 to 1023, ...) at most 8 rows name the same one
- face_angles: float32 [2, 131072], P(None, 'blk'), may hold values from -3.140625 to 3.140625
- face_height: float32 [131072], P('blk'), may hold values from 0.05 to 0.5
- wall_temp: float32 [131072], P('blk'), may hold values from -6 to 6
- face_visc: float32 [131072], P('blk'), may hold values from 0.005 to 0.05
Outputs:
- final_state: float32 [4, 2048, 128, 256], P(None, 'blk')
- wall_flux: float32 [4, 65536], P(None, 'blk')
Inputs may be any that keep to these rules, and one draw needn't show every extreme that they name: `sample_cell`: index i * 128 * 256 + j * 256 + k with i < 15, j < 127, k < 255, so that the whole block lies in the partition. `sample_owner`: among the 512 exchange points of one partition no owner is named more than 8 times, a bound that some block reaches.
All inputs are finite; a program needn't handle non-finite values.
Results may differ from a plain program's by a relative error of at most 0.0003.
Values sent between devices are 32-bit elements; how exact they have to be, the bound alone decides.
No kernel may reach another device: no remote copies, remote signals or barrier semaphores. Data moves between devices by JAX's collectives and lax.ppermute only.
A program may use at most 128 MiB of HBM per device.

v0:
```python
import jax
import jax.numpy as jnp
from jax import lax
from jax.sharding import PartitionSpec as P

NPTS = 64
NEWTON = 3
time_step = 0.1
grid_viscosity = 0.2
karman = 0.41
prandtl = 0.72
turb_prandtl = 0.9
speed_floor = 0.5


def extended(cells, sides, width):
    for axis, dim in sides:
        count = lax.axis_size(axis)
        head = lax.slice_in_dim(cells, 0, width, axis=dim)
        tail = lax.slice_in_dim(cells, cells.shape[dim] - width, cells.shape[dim], axis=dim)
        cells = jnp.concatenate(
            [
                lax.ppermute(tail, axis, [(i, (i + 1) % count) for i in range(count)]),
                cells,
                lax.ppermute(head, axis, [((i + 1) % count, i) for i in range(count)]),
            ],
            axis=dim,
        )
    return cells


def transport(padded):
    center = padded[:, 1:-1]
    velocity = center[0:3]
    framed = jnp.pad(center, ((0, 0), (0, 0), (1, 1), (1, 1)))
    east_side = padded[:, 2:]
    west_side = padded[:, :-2]
    north_side = framed[:, :, 2:, 1:-1]
    south_side = framed[:, :, :-2, 1:-1]
    upper_side = framed[:, :, 1:-1, 2:]
    lower_side = framed[:, :, 1:-1, :-2]
    advect = (
        velocity[0] * (east_side - west_side)
        + velocity[1] * (north_side - south_side)
        + velocity[2] * (upper_side - lower_side)
    )
    spread = (
        east_side + west_side + north_side + south_side + upper_side + lower_side - 6.0 * center
    )
    return -0.5 * advect + grid_viscosity * spread


def with_rims(field):
    return extended(field, (("blk", 1),), 1)


def corner_factor(fraction, upper_flag):
    if upper_flag:
        return fraction
    return 1.0 - fraction


def sample_lines(middle, sample_cell, sample_frac):
    span_cells = middle.shape[2]
    line_cells = middle.shape[3]
    points = sample_cell.shape[0]
    lines = middle.reshape(4, -1, line_cells)
    base_line = sample_cell // line_cells
    offset = sample_cell - base_line * line_cells
    line_ids = []
    plane_weights = []
    for step_x in (0, 1):
        for step_y in (0, 1):
            line_ids.append(base_line + step_x * span_cells + step_y)
            plane_weights.append(
                corner_factor(sample_frac[0], step_x) * corner_factor(sample_frac[1], step_y)
            )
    line_ids = jnp.stack(line_ids).reshape(-1)
    plane_weights = jnp.stack(plane_weights)
    picked = jnp.take(lines, line_ids, axis=1).reshape(4, 4, points, line_cells)
    along = lax.broadcasted_iota(jnp.int32, (points, line_cells), 1)
    lower_hit = (along == offset[:, None]).astype(jnp.float32)
    upper_hit = (along == offset[:, None] + 1).astype(jnp.float32)
    depth_weights = (
        lower_hit * (1.0 - sample_frac[2])[:, None] + upper_hit * sample_frac[2][:, None]
    )
    along_line = jnp.sum(picked * depth_weights[None, None], axis=3)
    return jnp.sum(along_line * plane_weights[None], axis=1)


def slot_index(owners, groups, capacity):
    onehot = (owners[:, None] == jnp.arange(groups, dtype=jnp.int32)[None, :]).astype(jnp.int32)
    before = jnp.cumsum(onehot, axis=0) - onehot
    position = jnp.sum(before * onehot, axis=1)
    return owners * capacity + position


def pick_slots(table, slot_table):
    return lax.dot_general(
        table,
        slot_table,
        (((1,), (1,)), ((), ())),
        precision=lax.Precision.HIGHEST,
        preferred_element_type=jnp.float32,
    )


def wall_model(sample, angles, height, wall_temp, viscosity):
    normal = jnp.stack(
        [
            jnp.sin(angles[0]) * jnp.cos(angles[1]),
            jnp.sin(angles[0]) * jnp.sin(angles[1]),
            jnp.cos(angles[0]),
        ]
    )
    normal_speed = jnp.sum(sample[0:3] * normal, axis=0)
    tangent = sample[0:3] - normal_speed[None] * normal
    tangent_speed = jnp.maximum(jnp.sqrt(jnp.sum(tangent * tangent, axis=0)), speed_floor)
    direction = tangent / tangent_speed[None]
    ladder = (jnp.arange(NPTS, dtype=jnp.float32) + 0.5) / NPTS
    heights = height[None] * (ladder * ladder)[:, None]
    quad_weights = height[None] * (2.0 * ladder / NPTS)[:, None]
    friction = jnp.sqrt(viscosity * tangent_speed / height)
    for newton_step in range(NEWTON):
        eddy_visc = viscosity[None] + karman * heights * friction[None]
        inverse_sum = jnp.sum(quad_weights / eddy_visc, axis=0)
        slope_sum = jnp.sum(quad_weights * karman * heights / (eddy_visc * eddy_visc), axis=0)
        residual = friction * friction * inverse_sum - tangent_speed
        derivative = 2.0 * friction * inverse_sum - friction * friction * slope_sum
        friction = friction - residual / derivative
    conduct = viscosity[None] / prandtl + karman * heights * friction[None] / turb_prandtl
    resist = jnp.sum(quad_weights / conduct, axis=0)
    heat_flux = (sample[3] - wall_temp) / resist
    stress = (friction * friction)[None] * direction
    return jnp.concatenate([stress, heat_flux[None]], axis=0)


def on_device(
    state, sample_cell, sample_frac, sample_owner, face_angles, face_height, wall_temp, face_visc
):
    groups = lax.axis_size("blk")
    capacity = face_height.shape[0] // groups
    middle = state + time_step * transport(with_rims(state))
    final_state = 0.5 * state + 0.5 * (middle + time_step * transport(with_rims(middle)))
    sampled = sample_lines(middle, sample_cell, sample_frac)
    slots = slot_index(sample_owner[:, 0], groups, capacity)
    slot_table = (slots[:, None] == jnp.arange(groups * capacity, dtype=jnp.int32)[None, :]).astype(
        jnp.float32
    )
    outgoing = jnp.dot(
        sampled, slot_table, precision=lax.Precision.HIGHEST, preferred_element_type=jnp.float32
    )
    incoming = lax.all_to_all(outgoing, "blk", split_axis=1, concat_axis=1, tiled=True)
    solved = wall_model(incoming, face_angles, face_height, wall_temp, face_visc)
    returned = lax.all_to_all(solved, "blk", split_axis=1, concat_axis=1, tiled=True)
    wall_flux = pick_slots(returned, slot_table)
    return (final_state, wall_flux)


def solution(mesh):
    placed = (
        P(None, "blk", None, None),
        P("blk"),
        P(None, "blk"),
        P("blk", None),
        P(None, "blk"),
        P("blk"),
        P("blk"),
        P("blk"),
    )
    return jax.shard_map(
        on_device,
        mesh=mesh,
        in_specs=placed,
        out_specs=(P(None, "blk", None, None), P(None, "blk")),
        check_vma=False,
    )
```

profile of v0, /device:TPU:1, one launch (start us, length us, event | category | flops | bytes accessed | tf_op | source)
XLA Modules:
  0.0 188.3 jit_solution(6805822651793586209)
XLA Ops:
  0.6 2.3 %fusion.37 = (f32[4,1,128,256]{3,2,1,0:T(8,128)}, f32[4,1,128,256]{3,2,1,0:T(8,128)}) fusion(f32[4,16,128,256]{3,2,1,0:T(8,128)} %param.8), kind=kLoop, calls=%fused_computation.128 | loop fusion | bytes 2097152 | tf_op jit(solution)/shard_map/slice | solution.py:20
  2.9 1.4 collective-permute-start
  4.3 1.3 collective-permute-start.1
  5.6 0.7 broadcast_add_fusion.3
  6.4 0.8 subtract_multiply_fusion.1
  7.2 0.8 copy.62
  8.3 0.9 fusion.25
  9.2 0.7 multiply_add_fusion.2
  9.9 1.0 cosine_reduce_fusion
  11.3 0.3 select_add_fusion
  11.7 5.6 %slice_bitcast_fusion.5 = (f32[16,128,256]{2,1,0:T(8,128)S(1)}, f32[16,128,256]{2,1,0:T(8,128)}, f32[16,128,256]{2,1,0:T(8,128)}) fusion(f32[4,16,128,256]{3,2,1,0:T(8,128)} %param.8), kind=kLoop, calls=%fused_computation.22 | loop fusion | bytes 12582912 | tf_op jit(solution)/shard_map/mul | solution.py:43
  17.3 26.2 %multiply_add_fusion = f32[4,16,128,256]{3,2,1,0:T(8,128)} fusion(f32[4,16,128,256]{3,2,1,0:T(8,128)} %param.8, f32[4,1,128,256]{3,2,1,0:T(8,128)S(1)} %collective-permute-done, f32[4,1,128,256]{3,2,1,0:T(8,128)} %collective-permute-done.1, f32[16,128,256]{2,1,0:T(8,128)} %get-tuple-element.26, f32[16,128,256]{2,1,0:T(8,128)} %get-tuple-element.27, ...), kind=kLoop, calls=%fused_computation.15 | loop fusion | flops 46137344 | bytes 24117248 | tf_op jit(solution)/shard_map/add | solution.py:143
  43.4 12.4 %copy.60 = f32[4,16,128,256]{3,0,2,1:T(4,128)} copy(f32[4,16,128,256]{3,2,1,0:T(8,128)} %multiply_add_fusion) | data formatting | bytes 16777216 | tf_op jit(solution)/shard_map/add | solution.py:143
  55.8 22.2 %gather_fusion = f32[2048,4,256]{2,1,0:T(4,128)} fusion(f32[4,2048,256]{2,0,1:T(4,128)} %bitcast.53, s32[2048]{0:T(1024)S(1)} %broadcast_clamp_fusion), kind=kCustom, calls=%fused_computation | custom fusion | bytes 16785408 | tf_op jit(solution)/shard_map/jit(_take)/gather | solution.py:80
  78.1 30.1 %multiply_reduce_fusion = f32[2048,4]{1,0:T(8,128)S(1)} fusion(f32[2048,4,256]{2,1,0:T(4,128)} %gather_fusion, f32[2048,256]{1,0:T(8,128)S(1)} %bitcast.54, pred[2048]{0:T(1024)(128)(4,1)S(1)} %compare_and_fusion), kind=kLoop, calls=%fused_computation.13 | loop fusion | flops 6283264 | bytes 10520576 | tf_op jit(solution)/shard_map/reduce_sum | solution.py:87
  108.2 0.3 copy.61
  108.6 1.0 fusion.1
  109.7 0.9 copy.64
  110.5 15.0 %all-to-all-start = ((f32[4,128,8]{2,0,1:T(4,128)}), f32[4,128,8]{2,0,1:T(4,128)S(1)}, u32[]{:S(2)}, u32[]{:S(2)}) async-start(f32[4,128,8]{2,0,1:T(4,128)} %copy.64), calls=%async_computation | async-start | bytes 524288 | tf_op jit(solution)/shard_map/all_to_all | solution.py:153
  125.5 2.3 %fusion.36 = (f32[4,1,128,256]{3,2,1,0:T(8,128)}, f32[4,1,128,256]{3,2,1,0:T(8,128)}) fusion(f32[4,16,128,256]{3,2,1,0:T(8,128)} %multiply_add_fusion), kind=kLoop, calls=%fused_computation.127 | loop fusion | bytes 2097152 | tf_op jit(solution)/shard_map/slice | solution.py:20
  127.8 1.1 collective-permute-start.2
  128.9 0.7 collective-permute-start.3
  129.6 7.0 %all-to-all-done = f32[4,128,8]{2,0,1:T(4,128)S(1)} async-done(((f32[4,128,8]{2,0,1:T(4,128)}), f32[4,128,8]{2,0,1:T(4,128)S(1)}, u32[]{:S(2)}, u32[]{:S(2)}) %all-to-all-start) | async-done | bytes 16416 | tf_op jit(solution)/shard_map/all_to_all | solution.py:153
  137.0 0.2 fusion.11
  137.3 0.2 fusion.15
  137.5 0.2 fusion.19
  138.5 0.9 copy.69
  139.4 7.4 %all-to-all-start.1 = ((f32[4,128,8]{2,0,1:T(4,128)}), f32[4,128,8]{2,0,1:T(4,128)S(1)}, u32[]{:S(2)}, u32[]{:S(2)}) async-start(f32[4,128,8]{2,0,1:T(4,128)} %copy.69), calls=%async_computation.1 | async-start | bytes 524288 | tf_op jit(solution)/shard_map/all_to_all | solution.py:155
  146.8 5.5 %slice_bitcast_fusion.2 = (f32[16,128,256]{2,1,0:T(8,128)S(1)}, f32[16,128,256]{2,1,0:T(8,128)}, f32[16,128,256]{2,1,0:T(8,128)}) fusion(f32[4,16,128,256]{3,2,1,0:T(8,128)} %multiply_add_fusion), kind=kLoop, calls=%fused_computation.18 | loop fusion | bytes 12582912 | tf_op jit(solution)/shard_map/mul | solution.py:43
  152.2 5.6 %all-to-all-done.1 = f32[4,128,8]{2,0,1:T(4,128)S(1)} async-done(((f32[4,128,8]{2,0,1:T(4,128)}), f32[4,128,8]{2,0,1:T(4,128)S(1)}, u32[]{:S(2)}, u32[]{:S(2)}) %all-to-all-start.1) | async-done | bytes 16416 | tf_op jit(solution)/shard_map/all_to_all | solution.py:155
  158.0 1.7 fusion
  159.7 28.5 %add_multiply_fusion = f32[4,16,128,256]{3,2,1,0:T(8,128)} fusion(f32[4,16,128,256]{3,2,1,0:T(8,128)} %param.8, f32[4,16,128,256]{3,2,1,0:T(8,128)} %multiply_add_fusion, f32[4,1,128,256]{3,2,1,0:T(8,128)S(1)} %collective-permute-done.2, f32[4,1,128,256]{3,2,1,0:T(8,128)} %collective-permute-done.3, f32[16,128,256]{2,1,0:T(8,128)} %get-tuple-element.22, ...), kind=kLoop, calls=%fused_computation.14 | loop fusion | flops 50331648 | bytes 32505856 | tf_op jit(solution)/shard_map/add | solution.py:144
  (57 shorter events, 2.1 us)
Async XLA Ops:
  2.9 14.3 %collective-permute-start = (f32[4,1,128,256]{3,2,1,0:T(8,128)}, f32[4,1,128,256]{3,2,1,0:T(8,128)S(1)}, u32[]{:S(2)}, u32[]{:S(2)}) collective-permute-start(f32[4,1,128,256]{3,2,1,0:T(8,128)} %get-tuple-element.29), channel_id=1, source_target_pairs={{1,0},{2,1},{3,2},{4,3},{5,4},{6,5},{7,6},{8,7},{9,8},{10,9},{11,1... | collective-permute-start | bytes 1572872 | tf_op jit(solution)/shard_map/ppermute | solution.py:25
  4.3 12.9 %collective-permute-start.1 = (f32[4,1,128,256]{3,2,1,0:T(8,128)}, f32[4,1,128,256]{3,2,1,0:T(8,128)}, u32[]{:S(2)}, u32[]{:S(2)}) collective-permute-start(f32[4,1,128,256]{3,2,1,0:T(8,128)} %get-tuple-element.28), channel_id=1, source_target_pairs={{0,1},{1,2},{2,3},{3,4},{4,5},{5,6},{6,7},{7,8},{8,9},{9,10},{10,1... | collective-permute-start | bytes 1572872 | tf_op jit(solution)/shard_map/ppermute | solution.py:23
  78.1 58.9 %copy-start = (f32[1024]{0:T(1024)S(1)}, f32[1024]{0:T(1024)}, u32[]{:S(2)}) copy-start(f32[1024]{0:T(1024)} %param.13) | copy-start | bytes 12292
  78.1 58.9 %copy-start.1 = (f32[1024]{0:T(1024)S(1)}, f32[1024]{0:T(1024)}, u32[]{:S(2)}) copy-start(f32[1024]{0:T(1024)} %param.15) | copy-start | bytes 12292
  78.1 60.2 %copy-start.2 = (f32[1024]{0:T(1024)S(1)}, f32[1024]{0:T(1024)}, u32[]{:S(2)}) copy-start(f32[1024]{0:T(1024)} %param.14) | copy-start | bytes 12292
  110.5 26.1 %all-to-all-start = ((f32[4,128,8]{2,0,1:T(4,128)}), f32[4,128,8]{2,0,1:T(4,128)S(1)}, u32[]{:S(2)}, u32[]{:S(2)}) async-start(f32[4,128,8]{2,0,1:T(4,128)} %copy.64), calls=%async_computation | async-start | bytes 524288 | tf_op jit(solution)/shard_map/all_to_all | solution.py:153
  127.8 31.9 %collective-permute-start.2 = (f32[4,1,128,256]{3,2,1,0:T(8,128)}, f32[4,1,128,256]{3,2,1,0:T(8,128)S(1)}, u32[]{:S(2)}, u32[]{:S(2)}) collective-permute-start(f32[4,1,128,256]{3,2,1,0:T(8,128)} %get-tuple-element.24), channel_id=1, source_target_pairs={{1,0},{2,1},{3,2},{4,3},{5,4},{6,5},{7,6},{8,7},{9,8},{10,9},{11,1... | collective-permute-start | bytes 1572872 | tf_op jit(solution)/shard_map/ppermute | solution.py:25
  128.9 30.8 %collective-permute-start.3 = (f32[4,1,128,256]{3,2,1,0:T(8,128)}, f32[4,1,128,256]{3,2,1,0:T(8,128)}, u32[]{:S(2)}, u32[]{:S(2)}) collective-permute-start(f32[4,1,128,256]{3,2,1,0:T(8,128)} %get-tuple-element.23), channel_id=1, source_target_pairs={{0,1},{1,2},{2,3},{3,4},{4,5},{5,6},{6,7},{7,8},{8,9},{9,10},{10,1... | collective-permute-start | bytes 1572872 | tf_op jit(solution)/shard_map/ppermute | solution.py:23
  139.4 18.5 %all-to-all-start.1 = ((f32[4,128,8]{2,0,1:T(4,128)}), f32[4,128,8]{2,0,1:T(4,128)S(1)}, u32[]{:S(2)}, u32[]{:S(2)}) async-start(f32[4,128,8]{2,0,1:T(4,128)} %copy.69), calls=%async_computation.1 | async-start | bytes 524288 | tf_op jit(solution)/shard_map/all_to_all | solution.py:155
where the time goes:
time: 189 us; the launch traced here: 188 us
  other arithmetic  90.7 us (48%)
  local copies, waits for them, and re-layouts  54.4 us (29%)
  starting transfers between devices  26.8 us (14%)
  waiting for transfers between devices  12.7 us (7%)
  matrix products  2.73 us (1%)
    reduce_sum x1, other arithmetic, sample_lines(): along_line = jnp.sum(picked * depth_weights[None, None], axis=3)  30.1 us
    add x1, other arithmetic, on_device(): 0.5 * state + 0.5 * (middle + time_step * transport(with_rims(middle)))  28.5 us
    add x1, other arithmetic, on_device(): middle = state + time_step * transport(with_rims(state))  26.2 us
    gather x1, local copies, waits for them, and re-layouts, sample_lines(): picked = jnp.take(lines, line_ids, axis=1).reshape(4, 4, points, line_cells)  22.2 us
    all_to_all x1, starting transfers between devices, on_device(): lax.all_to_all(outgoing, 'blk', split_axis=1, concat_axis=1, tiled=True)  15 us
    add x1, local copies, waits for them, and re-layouts, on_device(): middle = state + time_step * transport(with_rims(state))  12.4 us
    mul x2, local copies, waits for them, and re-layouts, transport(): velocity[0] * (east_side - west_side)  11.1 us
    all_to_all x1, starting transfers between devices, on_device(): lax.all_to_all(solved, 'blk', split_axis=1, concat_axis=1, tiled=True)  7.38 us
  transfers between devices with their start and end apart: 6, of which 2 were waited for; matrix products, arithmetic and copies ran while one was open for 13% of the time, Pallas kernels for 0%

commit v1 on v0

--- a/solution.py
+++ b/solution.py
@@ -152,7 +152,9 @@
     )
     incoming = lax.all_to_all(outgoing, "blk", split_axis=1, concat_axis=1, tiled=True)
     solved = wall_model(incoming, face_angles, face_height, wall_temp, face_visc)
-    returned = lax.all_to_all(solved, "blk", split_axis=1, concat_axis=1, tiled=True)
+    low = jnp.stack(jnp.split(solved, lax.axis_size("blk"), axis=1))
+    heard = lax.all_to_all(low, "blk", 0, 0)
+    returned = jnp.concatenate(heard, axis=1)
     wall_flux = pick_slots(returned, slot_table)
     return (final_state, wall_flux)
 

time: 189 us -> 273 us (1.44)
  other arithmetic: 90.7 us -> 175 us
    unnamed x1 -> x128, other arithmetic: 0.02 us -> 82.3 us
  transfers between devices with their start and end apart: 6 -> 6, of which waited for: 2 -> 2; matrix products, arithmetic and copies ran while one was open for 13% -> 39% of each run, Pallas kernels for 0% -> 0%
where the time goes in v1:
time: 273 us; the launch traced here: 272 us
  other arithmetic  175 us (64%)
  local copies, waits for them, and re-layouts  54.5 us (20%)
  starting transfers between devices  26.8 us (10%)
  waiting for transfers between devices  12.7 us (5%)
  matrix products  2.73 us (1%)
    unnamed x128, other arithmetic  82.3 us
    reduce_sum x1, other arithmetic, sample_lines(): along_line = jnp.sum(picked * depth_weights[None, None], axis=3)  30.1 us
    add x1, other arithmetic, on_device(): 0.5 * state + 0.5 * (middle + time_step * transport(with_rims(middle)))  28.6 us
    add x1, other arithmetic, on_device(): middle = state + time_step * transport(with_rims(state))  26.3 us
    gather x1, local copies, waits for them, and re-layouts, sample_lines(): picked = jnp.take(lines, line_ids, axis=1).reshape(4, 4, points, line_cells)  22.2 us
    all_to_all x1, starting transfers between devices, on_device(): lax.all_to_all(outgoing, 'blk', split_axis=1, concat_axis=1, tiled=True)  15 us
    add x1, local copies, waits for them, and re-layouts, on_device(): middle = state + time_step * transport(with_rims(state))  12.4 us
    mul x2, local copies, waits for them, and re-layouts, transport(): velocity[0] * (east_side - west_side)  11.1 us
  transfers between devices with their start and end apart: 6, of which 2 were waited for; matrix products, arithmetic and copies ran while one was open for 39% of the time, Pallas kernels for 0%

profile of v1, /device:TPU:1, one launch (start us, length us, event | category | flops | bytes accessed | tf_op | source)
XLA Modules:
  0.0 272.2 jit_solution(80384556576318408)
XLA Ops:
  0.6 2.3 fusion.171
  2.9 1.4 collective-permute-start
  4.3 1.3 collective-permute-start.1
  5.6 0.7 broadcast_add_fusion.3
  6.4 0.8 subtract_multiply_fusion.1
  7.2 0.8 copy.332
  8.3 0.9 fusion.25
  9.2 0.7 multiply_add_fusion.2
  10.4 1.7 slice_cosine_fusion
  13.0 5.6 %slice_bitcast_fusion.5 = (f32[16,128,256]{2,1,0:T(8,128)S(1)}, f32[16,128,256]{2,1,0:T(8,128)}, f32[16,128,256]{2,1,0:T(8,128)}) fusion(f32[4,16,128,256]{3,2,1,0:T(8,128)} %param.8), kind=kLoop, calls=%fused_computation.22 | loop fusion | bytes 12582912 | tf_op jit(solution)/shard_map/mul | solution.py:43
  18.6 26.3 %multiply_add_fusion = f32[4,16,128,256]{3,2,1,0:T(8,128)} fusion(f32[4,16,128,256]{3,2,1,0:T(8,128)} %param.8, f32[4,1,128,256]{3,2,1,0:T(8,128)S(1)} %collective-permute-done, f32[4,1,128,256]{3,2,1,0:T(8,128)} %collective-permute-done.1, f32[16,128,256]{2,1,0:T(8,128)} %get-tuple-element.27, f32[16,128,256]{2,1,0:T(8,128)} %get-tuple-element.28, ...), kind=kLoop, calls=%fused_computation.15 | loop fusion | flops 46137344 | bytes 24117248 | tf_op jit(solution)/shard_map/add | solution.py:143
  44.9 12.4 %copy.330 = f32[4,16,128,256]{3,0,2,1:T(4,128)} copy(f32[4,16,128,256]{3,2,1,0:T(8,128)} %multiply_add_fusion) | data formatting | bytes 16777216 | tf_op jit(solution)/shard_map/add | solution.py:143
  57.2 22.2 %gather_fusion = f32[2048,4,256]{2,1,0:T(4,128)} fusion(f32[4,2048,256]{2,0,1:T(4,128)} %bitcast.441, s32[2048]{0:T(1024)S(1)} %broadcast_clamp_fusion), kind=kCustom, calls=%fused_computation | custom fusion | bytes 16785408 | tf_op jit(solution)/shard_map/jit(_take)/gather | solution.py:80
  79.6 30.1 %multiply_reduce_fusion = f32[2048,4]{1,0:T(8,128)S(1)} fusion(f32[2048,4,256]{2,1,0:T(4,128)} %gather_fusion, f32[2048,256]{1,0:T(8,128)S(1)} %bitcast.442, pred[2048]{0:T(1024)(128)(4,1)S(1)} %compare_and_fusion), kind=kLoop, calls=%fused_computation.13 | loop fusion | flops 6283264 | bytes 10520576 | tf_op jit(solution)/shard_map/reduce_sum | solution.py:87
  110.1 1.0 fusion.1
  111.2 0.9 copy.334
  112.0 15.0 %all-to-all-start = ((f32[4,128,8]{2,0,1:T(4,128)}), f32[4,128,8]{2,0,1:T(4,128)S(1)}, u32[]{:S(2)}, u32[]{:S(2)}) async-start(f32[4,128,8]{2,0,1:T(4,128)} %copy.334), calls=%async_computation | async-start | bytes 524288 | tf_op jit(solution)/shard_map/all_to_all | solution.py:153
  127.0 2.3 fusion.170
  129.3 1.1 collective-permute-start.2
  130.4 0.7 collective-permute-start.3
  131.0 7.0 %all-to-all-done = f32[4,128,8]{2,0,1:T(4,128)S(1)} async-done(((f32[4,128,8]{2,0,1:T(4,128)}), f32[4,128,8]{2,0,1:T(4,128)S(1)}, u32[]{:S(2)}, u32[]{:S(2)}) %all-to-all-start) | async-done | bytes 16416 | tf_op jit(solution)/shard_map/all_to_all | solution.py:153
  152.4 0.7 constant_dynamic-update-slice_fusion.108
  173.9 0.7 constant_dynamic-update-slice_fusion.75
  185.5 0.7 constant_dynamic-update-slice_fusion.57
  194.5 0.7 constant_dynamic-update-slice_fusion.43
  195.8 0.7 constant_dynamic-update-slice_fusion.41
  222.5 0.7 constant_dynamic-update-slice_fusion
  223.2 7.4 %all-to-all-start.1 = ((f32[128,4,8]{2,1,0:T(4,128)}), f32[128,4,8]{2,1,0:T(4,128)S(1)}, u32[]{:S(2)}, u32[]{:S(2)}) async-start(f32[128,4,8]{2,1,0:T(4,128)} %constant_dynamic-update-slice_fusion), calls=%async_computation.1 | async-start | bytes 524288 | tf_op jit(solution)/shard_map/all_to_all | solution.py:156
  230.5 5.5 %slice_bitcast_fusion.2 = (f32[16,128,256]{2,1,0:T(8,128)S(1)}, f32[16,128,256]{2,1,0:T(8,128)}, f32[16,128,256]{2,1,0:T(8,128)}) fusion(f32[4,16,128,256]{3,2,1,0:T(8,128)} %multiply_add_fusion), kind=kLoop, calls=%fused_computation.18 | loop fusion | bytes 12582912 | tf_op jit(solution)/shard_map/mul | solution.py:43
  236.0 5.6 %all-to-all-done.1 = f32[128,4,8]{2,1,0:T(4,128)S(1)} async-done(((f32[128,4,8]{2,1,0:T(4,128)}), f32[128,4,8]{2,1,0:T(4,128)S(1)}, u32[]{:S(2)}, u32[]{:S(2)}) %all-to-all-start.1) | async-done | bytes 16416 | tf_op jit(solution)/shard_map/all_to_all | solution.py:156
  241.8 1.7 fusion
  243.5 28.6 %add_multiply_fusion = f32[4,16,128,256]{3,2,1,0:T(8,128)} fusion(f32[4,16,128,256]{3,2,1,0:T(8,128)} %param.8, f32[4,16,128,256]{3,2,1,0:T(8,128)} %multiply_add_fusion, f32[4,1,128,256]{3,2,1,0:T(8,128)S(1)} %collective-permute-done.2, f32[4,1,128,256]{3,2,1,0:T(8,128)} %collective-permute-done.3, f32[16,128,256]{2,1,0:T(8,128)} %get-tuple-element.23, ...), kind=kLoop, calls=%fused_computation.14 | loop fusion | flops 50331648 | bytes 32505856 | tf_op jit(solution)/shard_map/add | solution.py:144
  (186 shorter events, 83.3 us)
Async XLA Ops:
  2.9 15.7 %collective-permute-start = (f32[4,1,128,256]{3,2,1,0:T(8,128)}, f32[4,1,128,256]{3,2,1,0:T(8,128)S(1)}, u32[]{:S(2)}, u32[]{:S(2)}) collective-permute-start(f32[4,1,128,256]{3,2,1,0:T(8,128)} %get-tuple-element.30), channel_id=1, source_target_pairs={{1,0},{2,1},{3,2},{4,3},{5,4},{6,5},{7,6},{8,7},{9,8},{10,9},{11,1... | collective-permute-start | bytes 1572872 | tf_op jit(solution)/shard_map/ppermute | solution.py:25
  4.3 14.3 %collective-permute-start.1 = (f32[4,1,128,256]{3,2,1,0:T(8,128)}, f32[4,1,128,256]{3,2,1,0:T(8,128)}, u32[]{:S(2)}, u32[]{:S(2)}) collective-permute-start(f32[4,1,128,256]{3,2,1,0:T(8,128)} %get-tuple-element.29), channel_id=1, source_target_pairs={{0,1},{1,2},{2,3},{3,4},{4,5},{5,6},{6,7},{7,8},{8,9},{9,10},{10,1... | collective-permute-start | bytes 1572872 | tf_op jit(solution)/shard_map/ppermute | solution.py:23
  79.6 58.9 %copy-start = (f32[1024]{0:T(1024)S(1)}, f32[1024]{0:T(1024)}, u32[]{:S(2)}) copy-start(f32[1024]{0:T(1024)} %param.13) | copy-start | bytes 12292
  79.6 58.9 %copy-start.1 = (f32[1024]{0:T(1024)S(1)}, f32[1024]{0:T(1024)}, u32[]{:S(2)}) copy-start(f32[1024]{0:T(1024)} %param.15) | copy-start | bytes 12292
  79.6 60.4 %copy-start.2 = (f32[1024]{0:T(1024)S(1)}, f32[1024]{0:T(1024)}, u32[]{:S(2)}) copy-start(f32[1024]{0:T(1024)} %param.14) | copy-start | bytes 12292
  112.0 26.1 %all-to-all-start = ((f32[4,128,8]{2,0,1:T(4,128)}), f32[4,128,8]{2,0,1:T(4,128)S(1)}, u32[]{:S(2)}, u32[]{:S(2)}) async-start(f32[4,128,8]{2,0,1:T(4,128)} %copy.334), calls=%async_computation | async-start | bytes 524288 | tf_op jit(solution)/shard_map/all_to_all | solution.py:153
  129.3 114.2 %collective-permute-start.2 = (f32[4,1,128,256]{3,2,1,0:T(8,128)}, f32[4,1,128,256]{3,2,1,0:T(8,128)S(1)}, u32[]{:S(2)}, u32[]{:S(2)}) collective-permute-start(f32[4,1,128,256]{3,2,1,0:T(8,128)} %get-tuple-element.25), channel_id=1, source_target_pairs={{1,0},{2,1},{3,2},{4,3},{5,4},{6,5},{7,6},{8,7},{9,8},{10,9},{11,1... | collective-permute-start | bytes 1572872 | tf_op jit(solution)/shard_map/ppermute | solution.py:25
  130.4 113.1 %collective-permute-start.3 = (f32[4,1,128,256]{3,2,1,0:T(8,128)}, f32[4,1,128,256]{3,2,1,0:T(8,128)}, u32[]{:S(2)}, u32[]{:S(2)}) collective-permute-start(f32[4,1,128,256]{3,2,1,0:T(8,128)} %get-tuple-element.24), channel_id=1, source_target_pairs={{0,1},{1,2},{2,3},{3,4},{4,5},{5,6},{6,7},{7,8},{8,9},{9,10},{10,1... | collective-permute-start | bytes 1572872 | tf_op jit(solution)/shard_map/ppermute | solution.py:23
  223.2 18.5 %all-to-all-start.1 = ((f32[128,4,8]{2,1,0:T(4,128)}), f32[128,4,8]{2,1,0:T(4,128)S(1)}, u32[]{:S(2)}, u32[]{:S(2)}) async-start(f32[128,4,8]{2,1,0:T(4,128)} %constant_dynamic-update-slice_fusion), calls=%async_computation.1 | async-start | bytes 524288 | tf_op jit(solution)/shard_map/all_to_all | solution.py:156
